TPU v7x, 32 devices: a whole 2x2x4 slice. The times are simulated.
32 devices in a mesh: groups: 2 (over y), seq: 8 (over z, x), tensor: 2 (over core).
Axes of the slice: x: 2, y: 2, z: 4, core: 2. Of those that a mesh axis runs over, the one named last changes fastest.
Arguments:
- queries: bfloat16 [256, 3072], P(('groups', 'seq'), 'tensor'), parts along dimension 0, may hold values from -8 to 8
- keys: bfloat16 [16384, 3072], P(('groups', 'seq'), 'tensor'), parts along dimension 0, may hold values from -8 to 8
- values: bfloat16 [16384, 3072], P(('groups', 'seq'), 'tensor'), parts along dimension 0, may hold values from -6 to 6
Outputs:
- context: bfloat16 [256, 3072], P(('groups', 'seq'), 'tensor'), parts along dimension 0
There are 2 independent parts, one for each index of `groups`. A program takes and returns all parts, laid end to end along the dimension named above; each array names one. Nothing has to cross between parts.
All inputs are finite; a program needn't handle non-finite values.
Results may differ from a plain program's by a relative error of at most 0.0029.
Values may be sent and summed in bfloat16 or wider, within the bound.
A program may use at most 64 MiB of HBM per device.

v0:
```python
import math

import jax
import jax.numpy as jnp
from jax import lax
from jax.sharding import PartitionSpec as P

HEAD_DIM = 256


def body(queries, keys, values):
    gathered = lax.all_gather(queries, "seq", axis=0, tiled=True)
    query_count = gathered.shape[0]
    heads_here = keys.shape[1] // HEAD_DIM
    score_factor = 1.0 / math.sqrt(HEAD_DIM)
    key_heads = keys.reshape(keys.shape[0], heads_here, HEAD_DIM)
    value_heads = values.reshape(values.shape[0], heads_here, HEAD_DIM)
    block_rows = min(512, query_count)
    query_blocks = gathered.reshape(query_count // block_rows, block_rows, heads_here, HEAD_DIM)

    def attend(query_block):
        scores = (
            jnp.einsum("qhd,khd->qhk", query_block, key_heads, preferred_element_type=jnp.float32)
            * score_factor
        )
        block_peak = jnp.max(scores, axis=-1)
        weights = jnp.exp(scores - block_peak[..., None])
        block_sums = jnp.sum(weights, axis=-1)
        block_context = jnp.einsum(
            "qhk,khd->qhd",
            weights.astype(jnp.bfloat16),
            value_heads,
            preferred_element_type=jnp.float32,
        )
        return (block_context, block_peak, block_sums)

    contexts, block_peaks, totals = lax.map(attend, query_blocks)
    contexts = contexts.reshape(query_count, heads_here * HEAD_DIM)
    block_peaks = block_peaks.reshape(query_count, heads_here)
    totals = totals.reshape(query_count, heads_here)
    owners = lax.axis_size("seq")
    own_rows = query_count // owners
    overall = lax.pmax(block_peaks, "seq")
    factor = jnp.exp(block_peaks - overall)
    scaled = (contexts.reshape(query_count, heads_here, HEAD_DIM) * factor[..., None]).reshape(
        query_count, heads_here * HEAD_DIM
    )
    numerator, denominator = (
        lax.psum_scatter(scaled, "seq", scatter_dimension=0, tiled=True),
        lax.psum_scatter(totals * factor, "seq", scatter_dimension=0, tiled=True),
    )
    numerator = numerator.reshape(own_rows, heads_here, HEAD_DIM)
    result = numerator / denominator[..., None]
    return result.reshape(own_rows, heads_here * HEAD_DIM).astype(jnp.bfloat16)


def solution(mesh):
    return jax.shard_map(
        body,
        mesh=mesh,
        in_specs=(
            P(("groups", "seq"), "tensor"),
            P(("groups", "seq"), "tensor"),
            P(("groups", "seq"), "tensor"),
        ),
        out_specs=P(("groups", "seq"), "tensor"),
        check_vma=False,
    )
```

profile of v0, /device:TPU:0, one launch (start us, length us, event | category | flops | bytes accessed | tf_op | source)
XLA Modules:
  0.0 201.9 jit_solution(4060918480793108735)
XLA Ops:
  6.5 0.0 copy-start
  6.5 0.0 reduce-scatter.9.cloned.1.call-start
  6.5 4.7 %copy.19 = bf16[1024,1536]{0,1:T(8,128)(2,1)} copy(bf16[1024,1536]{1,0:T(8,128)(2,1)} %param.4) | data formatting | bytes 6291456 | tf_op args[1]
  11.2 0.0 copy-done
  11.2 32.7 %all_gather.3 = bf16[128,1536]{1,0:T(8,128)(2,1)S(1)} all-gather(bf16[16,1536]{1,0:T(8,128)(2,1)S(1)} %copy-done), channel_id=1, replica_groups=mesh['groups'=2,'seq'=8,'tensor'=2] {'seq'}, dimensions={0}, use_global_device_ids=true | all-gather | bytes 442368 | tf_op jit(solution)/shard_map/all_gather | solution.py:12
  43.9 0.2 copy.20
  44.2 3.1 %bitcast_reduce_fusion = (f32[128,6]{0,1:T(8,128)S(1)}, f32[6,1024,128]{2,1,0:T(8,128)S(1)}) fusion(bf16[1024,6,256]{0,2,1:T(8,128)(2,1)} %bitcast.29, bf16[128,6,256]{0,2,1:T(8,128)(2,1)S(1)} %bitcast.32), kind=kOutput, calls=%fused_computation.1 | convolution fusion | flops 404225280 | bytes 6687744 | tf_op jit(solution)/shard_map/while/body/eval_jaxpr/qhd,khd->qhk/dot_general | solution.py:23
  47.3 21.4 %pmax.7 = f32[128,6]{0,1:T(8,128)S(1)} all-reduce(f32[128,6]{0,1:T(8,128)S(1)} %get-tuple-element.19), channel_id=1, replica_groups=mesh['groups'=2,'seq'=8,'tensor'=2] {'seq'}, use_global_device_ids=true, to_apply=%region_1.0 | all-reduce | flops 768 | bytes 6144 | tf_op jit(solution)/shard_map/pmax | solution.py:43
  68.7 0.5 fusion.1
  69.3 0.7 copy.35
  70.0 0.0 reduce-scatter.9.cloned.1.call-update
  70.0 0.0 reduce-scatter.7.cloned.1.call-start
  70.1 4.6 %copy.23 = bf16[1024,1536]{0,1:T(8,128)(2,1)} copy(bf16[1024,1536]{1,0:T(8,128)(2,1)} %param.5) | data formatting | bytes 6291456 | tf_op args[2]
  74.7 3.9 %fusion.10 = f32[128,6,256]{2,0,1:T(8,128)} fusion(bf16[1024,6,256]{0,2,1:T(8,128)(2,1)} %bitcast.30, f32[6,1024,128]{2,1,0:T(8,128)S(1)} %get-tuple-element.20, f32[128,6]{0,1:T(8,128)S(1)} %get-tuple-element.19, f32[128,6]{0,1:T(8,128)S(1)} %get-tuple-element.18), kind=kOutput, calls=%fused_computation.9 | convolution fusion | flops 405209088 | bytes 7084032 | tf_op jit(solution)/shard_map/while/body/eval_jaxpr/qhk,khd->qhd/dot_general | solution.py:29
  78.6 1.4 copy.26
  80.0 1.2 copy.33
  81.2 0.0 reduce-scatter.7.cloned.1.call-update
  81.2 47.5 %reduce-scatter.9.cloned.1.call-done = f32[16,6]{1,0:T(8,128)} async-done(((f32[128,6]{1,0:T(8,128)}), f32[16,6]{1,0:T(8,128)}) %reduce-scatter.9.cloned.1.call-update) | async-done | bytes 400 | tf_op jit(solution)/shard_map/reduce_scatter | solution.py:50
  128.7 0.8 div.11
  129.5 64.0 %reduce-scatter.7.cloned.1.call-done = f32[16,1536]{1,0:T(8,128)} async-done(((f32[128,1536]{1,0:T(8,128)}), f32[16,1536]{1,0:T(8,128)}) %reduce-scatter.7.cloned.1.call-update) | async-done | bytes 98320 | tf_op jit(solution)/shard_map/reduce_scatter | solution.py:49
  193.6 1.5 divide_convert_fusion
  (2 shorter events, 0.0 us)
Async XLA Ops:
  6.5 4.7 %copy-start = (bf16[16,1536]{1,0:T(8,128)(2,1)S(1)}, bf16[16,1536]{1,0:T(8,128)(2,1)}, u32[]{:S(2)}) copy-start(bf16[16,1536]{1,0:T(8,128)(2,1)} %param.3) | copy-start | bytes 147460
  6.5 122.2 %reduce-scatter.9.cloned.1.call-start = ((), (), s32[]{:S(2)}) async-start(), calls=%async_computation.3 | async-start | bytes 73728 | tf_op jit(solution)/shard_map/reduce_scatter | solution.py:50
  70.0 123.6 %reduce-scatter.7.cloned.1.call-start = ((), (), s32[]{:S(2)}) async-start(), calls=%async_computation.2 | async-start | bytes 884736 | tf_op jit(solution)/shard_map/reduce_scatter | solution.py:49
Sparse Core Ops, SparseCore 0:
  70.1 58.5 reduce-scatter.8
  132.0 61.5 reduce-scatter.6
where the time goes:
time: 202 us
  waiting for transfers between devices  112 us (55%)
  blocking collectives  54.2 us (27%)
  local copies, waits for them, and re-layouts  13.6 us (7%)
  between operations  13.4 us (7%)
  matrix products  7.05 us (3%)
  other arithmetic  2.06 us (1%)
    reduce_scatter x1, waiting for transfers between devices, body(): lax.psum_scatter(scaled, 'seq', scatter_dimension=0, tiled=True)  64 us
    reduce_scatter x1, waiting for transfers between devices, body(): lax.psum_scatter(totals * factor, 'seq', scatter_dimension=0, tiled=True)  47.5 us
    all_gather x1, blocking collectives, body(): gathered = lax.all_gather(queries, 'seq', axis=0, tiled=True)  32.7 us
    pmax x1, blocking collectives, body(): overall = lax.pmax(block_peaks, 'seq')  21.4 us
    unnamed x7, local copies, waits for them, and re-layouts  11.2 us
  transfers between devices with their start and end apart: 2, of which 2 were waited for; matrix products, arithmetic and copies ran while one was open for 6% of the time, Pallas kernels for 0%

commit v1 on v0

v1 whole, which is shorter than its diff:
```python
import functools
import math

import jax
import jax.numpy as jnp
from jax import lax
from jax.experimental import pallas as pl
from jax.experimental.pallas import tpu as pltpu
from jax.sharding import PartitionSpec as P

HEAD_DIM = 256
LANES = 128
LINK = jnp.bfloat16


def over(count, step):
    if count <= 16:
        for index in range(count):
            step(index)
    else:
        lax.fori_loop(0, count, lambda index, _: (step(index), 0)[1], 0)


def encode(x):
    squared = x * x
    return (squared * (x * jnp.abs(x))).astype(LINK)


def decode(y):
    y = y.astype(jnp.float32)
    root = jnp.sqrt(jnp.sqrt(jnp.abs(y)))
    return jnp.where(y < 0, -root, root)


def kernel(
    n, q_ref, k_hbm, v_hbm, o_ref, qall, kbuf, vbuf, ctx, stat, rctx, rstat,
    ksem, vsem, qsend, qrecv, csend, crecv, ssend, srecv,
):
    rows, columns = q_ref.shape
    heads = columns // HEAD_DIM
    factor = 1.0 / math.sqrt(HEAD_DIM)
    me = lax.axis_index("seq")

    def cols(h):
        return pl.ds(h * HEAD_DIM, HEAD_DIM)

    def k_copy(h):
        return pltpu.make_async_copy(k_hbm.at[:, cols(h)], kbuf.at[h], ksem.at[h])

    def v_copy(h):
        return pltpu.make_async_copy(v_hbm.at[:, cols(h)], vbuf.at[h], vsem.at[h])

    def peer(d):
        return {"seq": lax.rem(me + d + 1, n)}

    def source(d):
        return lax.rem(me + n - d - 1, n)

    def q_send(d):
        return pltpu.make_async_remote_copy(
            src_ref=q_ref, dst_ref=qall.at[me], send_sem=qsend.at[d], recv_sem=qrecv.at[d],
            device_id=peer(d), device_id_type=pl.DeviceIdType.MESH,
        )

    def c_send(d, h):
        return pltpu.make_async_remote_copy(
            src_ref=ctx.at[h, peer(d)["seq"]], dst_ref=rctx.at[h, me],
            send_sem=csend.at[h, d], recv_sem=crecv.at[h, d],
            device_id=peer(d), device_id_type=pl.DeviceIdType.MESH,
        )

    def s_send(d):
        return pltpu.make_async_remote_copy(
            src_ref=stat.at[peer(d)["seq"]], dst_ref=rstat.at[me],
            send_sem=ssend.at[d], recv_sem=srecv.at[d],
            device_id=peer(d), device_id_type=pl.DeviceIdType.MESH,
        )

    for h in range(heads):
        k_copy(h).start()
        v_copy(h).start()

    barrier = pltpu.get_barrier_semaphore()
    over(n - 1, lambda d: pl.semaphore_signal(
        barrier, inc=1, device_id=peer(d), device_id_type=pl.DeviceIdType.MESH))
    pl.semaphore_wait(barrier, n - 1)

    over(n - 1, lambda d: q_send(d).start())
    qall[me] = q_ref[...]
    over(n - 1, lambda d: q_send(d).wait_recv())

    group = min(n, 8)

    def attend(h, g):
        base = g * group
        query = qall[pl.ds(base, group), :, cols(h)].reshape(group * rows, HEAD_DIM)
        scores = lax.dot_general(
            query, kbuf[h], (((1,), (1,)), ((), ())), preferred_element_type=jnp.float32
        )
        peak = jnp.max(scores, axis=-1, keepdims=True)
        weights = jnp.exp((scores - peak) * factor)
        sums = jnp.sum(weights, axis=-1, keepdims=True)
        context = jnp.dot(
            weights.astype(jnp.bfloat16), vbuf[h], preferred_element_type=jnp.float32
        )
        size = jnp.max(jnp.abs(context), axis=-1, keepdims=True)
        size = jnp.maximum(size, 1e-30)
        ctx[h, pl.ds(base, group)] = encode(context / size).reshape(group, rows, HEAD_DIM)
        for place, value in ((0, peak * factor), (heads, sums), (2 * heads, size)):
            stat[pl.ds(base, group), :, pl.ds(place + h, 1)] = value.reshape(group, rows, 1)

    for h in range(heads):
        k_copy(h).wait()
        v_copy(h).wait()
        over(n // group, functools.partial(attend, h))
        over(n - 1, lambda d: c_send(d, h).start())
    over(n - 1, lambda d: s_send(d).start())
    rstat[me] = stat[me]
    for h in range(heads):
        rctx[h, me] = ctx[h, me]
    over(n - 1, lambda d: s_send(d).wait_recv())

    peaks = rstat[...]
    top = jnp.max(peaks, axis=0, keepdims=True)
    shrink = jnp.exp(peaks - top)
    for h in range(heads):
        over(n - 1, lambda d: c_send(d, h).wait_recv())
        part = shrink[:, :, h : h + 1]
        total = jnp.sum(part * peaks[:, :, heads + h : heads + h + 1], axis=0)
        scale = part * peaks[:, :, 2 * heads + h : 2 * heads + h + 1]
        numerator = jnp.sum(decode(rctx[h]) * scale, axis=0)
        o_ref[:, cols(h)] = (numerator / total).astype(o_ref.dtype)

    over(n - 1, lambda d: q_send(d).wait_send())
    over(n - 1, lambda d: s_send(d).wait_send())
    for h in range(heads):
        over(n - 1, lambda d: c_send(d, h).wait_send())


def body(n, queries, keys, values):
    rows, columns = queries.shape
    depth = keys.shape[0]
    heads = columns // HEAD_DIM
    dma = pltpu.SemaphoreType.DMA
    vmem = pl.BlockSpec(memory_space=pltpu.VMEM)
    return pl.pallas_call(
        functools.partial(kernel, n),
        out_shape=jax.ShapeDtypeStruct((rows, columns), jnp.bfloat16),
        in_specs=[vmem, pl.BlockSpec(memory_space=pl.ANY), pl.BlockSpec(memory_space=pl.ANY)],
        out_specs=vmem,
        scratch_shapes=[
            pltpu.VMEM((n, rows, columns), jnp.bfloat16),
            pltpu.VMEM((heads, depth, HEAD_DIM), jnp.bfloat16),
            pltpu.VMEM((heads, depth, HEAD_DIM), jnp.bfloat16),
            pltpu.VMEM((heads, n, rows, HEAD_DIM), LINK),
            pltpu.VMEM((n, rows, LANES), jnp.float32),
            pltpu.VMEM((heads, n, rows, HEAD_DIM), LINK),
            pltpu.VMEM((n, rows, LANES), jnp.float32),
            dma((heads,)), dma((heads,)),
            dma((n - 1,)), dma((n - 1,)),
            dma((heads, n - 1)), dma((heads, n - 1)),
            dma((n - 1,)), dma((n - 1,)),
        ],
        compiler_params=pltpu.CompilerParams(
            collective_id=0, has_side_effects=True, vmem_limit_bytes=48 * 1024 * 1024
        ),
        name="attend",
    )(queries, keys, values)


def solution(mesh):
    spec = P(("groups", "seq"), "tensor")
    return jax.shard_map(
        functools.partial(body, mesh.shape["seq"]),
        mesh=mesh,
        in_specs=(spec, spec, spec),
        out_specs=spec,
        check_vma=False,
    )
```

time: 202 us -> 32.4 us (0.16)
  waiting for transfers between devices: 112 us -> 0 us
  blocking collectives: 54.2 us -> 0 us
  Pallas kernels: 0 us -> 28.9 us
  between operations: 13.4 us -> 0.01 us
  local copies, waits for them, and re-layouts: 13.6 us -> 3.31 us
  matrix products: 7.05 us -> 0 us
  other arithmetic: 2.06 us -> 0 us
    reduce_scatter x2 -> x0, waiting for transfers between devices: 112 us -> none  [the longest x1 64 us: body(): lax.psum_scatter(scaled, 'seq', scatter_dimension=0, tiled=True)]
    all_gather x1 -> x0, blocking collectives: 32.7 us -> none  [body(): gathered = lax.all_gather(queries, 'seq', axis=0, tiled=True)]
    pallas_call x0 -> x1, Pallas kernels: none -> 28.9 us  [body(): pl.pallas_call(functools.partial(kernel, n), out_shape=jax.ShapeDtypeStru...]
    pmax x1 -> x0, blocking collectives: 21.4 us -> none  [body(): overall = lax.pmax(block_peaks, 'seq')]
    unnamed x7 -> x5, local copies, waits for them, and re-layouts: 11.2 us -> 3.31 us
    dot_general x2 -> x0, matrix products: 7.05 us -> none  [the longest x1 3.94 us: attend(): jnp.einsum('qhk,khd->qhd', weights.astype(jnp.bfloat16), value_heads, pre...]
  transfers between devices with their start and end apart: 2 -> 0, of which waited for: 2 -> 0; matrix products, arithmetic and copies ran while one was open for 6% -> 0% of each run, Pallas kernels for 0% -> 0%
where the time goes in v1:
time: 32.4 us; the launch traced here: 32.2 us
  Pallas kernels  28.9 us (89%)
  local copies, waits for them, and re-layouts  3.31 us (10%)
    pallas_call x1, Pallas kernels, body(): pl.pallas_call(functools.partial(kernel, n), out_shape=jax.ShapeDtypeStru...  28.9 us
    unnamed x5, local copies, waits for them, and re-layouts  3.31 us

profile of v1, /device:TPU:0, one launch (start us, length us, event | category | flops | bytes accessed | tf_op | source)
XLA Modules:
  0.0 32.2 jit_solution(11382680352396702217)
XLA Ops:
  0.0 0.0 copy-start
  0.0 1.9 %copy-done = bf16[1024,1536]{1,0:T(8,128)(2,1)S(1)} copy-done((bf16[1024,1536]{1,0:T(8,128)(2,1)S(1)}, bf16[1024,1536]{1,0:T(8,128)(2,1)}, u32[]{:S(2)}) %copy-start) | copy-done | bytes 3145752
  1.9 0.0 copy-start.1
  1.9 0.8 %copy-done.1 = bf16[16,1536]{1,0:T(8,128)(2,1)S(1)} copy-done((bf16[16,1536]{1,0:T(8,128)(2,1)S(1)}, bf16[16,1536]{1,0:T(8,128)(2,1)}, u32[]{:S(2)}) %copy-start.1) | copy-done | bytes 49176
  2.7 28.9 %attend.1 = bf16[16,1536]{1,0:T(8,128)(2,1)S(1)} custom-call(bf16[16,1536]{1,0:T(8,128)(2,1)S(1)} %copy-done.1, bf16[1024,1536]{1,0:T(8,128)(2,1)S(1)} %copy-done, bf16[1024,1536]{1,0:T(8,128)(2,1)} %v_hbm.1), custom_call_target="tpu_custom_call" | custom-call | tf_op jit(solution)/shard_map/attend/pallas_call | solution.py:146
  31.6 0.6 %copy.5 = bf16[16,1536]{1,0:T(8,128)(2,1)} copy(bf16[16,1536]{1,0:T(8,128)(2,1)S(1)} %attend.1) | data formatting | bytes 98304
Async XLA Ops:
  0.0 1.9 %copy-start = (bf16[1024,1536]{1,0:T(8,128)(2,1)S(1)}, bf16[1024,1536]{1,0:T(8,128)(2,1)}, u32[]{:S(2)}) copy-start(bf16[1024,1536]{1,0:T(8,128)(2,1)} %k_hbm.1) | copy-start | bytes 9437188
  1.9 0.8 %copy-start.1 = (bf16[16,1536]{1,0:T(8,128)(2,1)S(1)}, bf16[16,1536]{1,0:T(8,128)(2,1)}, u32[]{:S(2)}) copy-start(bf16[16,1536]{1,0:T(8,128)(2,1)} %q_ref.1) | copy-start | bytes 147460

commit v2 on v1

v2 whole, which is shorter than its diff:
```python
import functools
import math

import jax
import jax.numpy as jnp
from jax import lax
from jax.experimental import pallas as pl
from jax.experimental.pallas import tpu as pltpu
from jax.sharding import PartitionSpec as P

HEAD_DIM = 256
LANES = 128
LINK = jnp.bfloat16
CHUNK = 3
RAISE = 2.0**28
LOWER = 2.0**-28


def encode(x):
    x = x * RAISE
    squared = x * x
    return (squared * (x * jnp.abs(x))).astype(LINK)


def decode(y):
    y = y.astype(jnp.float32)
    root = jnp.sqrt(jnp.sqrt(jnp.abs(y))) * LOWER
    return jnp.where(y < 0, -root, root)


def over(start, stop, step):
    if stop - start <= 16:
        for index in range(start, stop):
            step(index)
    else:
        lax.fori_loop(start, stop, lambda index, _: (step(index), 0)[1], 0)


def kernel(
    n, q_ref, k_hbm, v_hbm, o_ref, qall, kbuf, vbuf, local, stat, xout, xin, tout, tin,
    zout, zin, zstat, ystat,
    ksem, vsem, qzs, qzr, qxs, qxr, xs, xr, ts, tr, zs, zr, ys, yr,
):
    rows, columns = q_ref.shape
    heads = columns // HEAD_DIM
    chunks = heads // CHUNK
    factor = 1.0 / math.sqrt(HEAD_DIM)
    m = n // 2
    me = lax.axis_index("seq")
    place = me // 2
    side = lax.rem(me, 2)
    other = 1 - side
    pair = 2 * place + other

    def ahead(k):
        return lax.rem(place + k, m)

    def behind(k):
        return lax.rem(place + m - k, m)

    def cols(h):
        return pl.ds(h * HEAD_DIM, HEAD_DIM)

    def span(c):
        return pl.ds(c * CHUNK * HEAD_DIM, CHUNK * HEAD_DIM)

    def k_copy(h):
        return pltpu.make_async_copy(k_hbm.at[:, cols(h)], kbuf.at[h], ksem.at[h])

    def v_copy(h):
        return pltpu.make_async_copy(v_hbm.at[:, cols(h)], vbuf.at[h], vsem.at[h])

    def remote(src, dst, send, recv, to):
        return pltpu.make_async_remote_copy(
            src_ref=src, dst_ref=dst, send_sem=send, recv_sem=recv,
            device_id={"seq": to}, device_id_type=pl.DeviceIdType.MESH,
        )

    def column(k):
        return 2 * ahead(k) + side

    def qz(c, k):
        return remote(q_ref.at[:, span(c)], qall.at[side, place, :, span(c)],
                      qzs.at[c, k], qzr.at[c, k], column(k))

    def qx_own(c):
        return remote(q_ref.at[:, span(c)], qall.at[side, place, :, span(c)],
                      qxs.at[c, 0], qxr.at[c, 0], pair)

    def qx(c, k):
        ref = qall.at[side, behind(k), :, span(c)]
        return remote(ref, ref, qxs.at[c, k], qxr.at[c, k], pair)

    def x_send(c):
        return remote(xout.at[c], xin.at[c], xs.at[c], xr.at[c], pair)

    def t_send(c):
        return remote(tout.at[c], tin.at[c], ts.at[c], tr.at[c], pair)

    def z_send(c, k):
        return remote(zout.at[c, ahead(k)], zin.at[c, place], zs.at[c, k], zr.at[c, k], column(k))

    def y_send(k):
        return remote(zstat.at[ahead(k)], ystat.at[place], ys.at[k], yr.at[k], column(k))

    barrier = pltpu.get_barrier_semaphore()

    def greet(to):
        pl.semaphore_signal(
            barrier, inc=1, device_id={"seq": to}, device_id_type=pl.DeviceIdType.MESH)

    over(1, m, lambda k: greet(column(k)))
    greet(pair)
    for h in range(heads):
        k_copy(h).start()
        v_copy(h).start()
    qall[side, place] = q_ref[...]
    stat[...] = jnp.zeros_like(stat)
    zstat[...] = jnp.zeros_like(zstat)
    pl.semaphore_wait(barrier, m)

    for c in range(chunks):
        over(1, m, lambda k: qz(c, k).start())
        qx_own(c).start()
    for h in range(heads):
        k_copy(h).wait()
        v_copy(h).wait()

    group = min(m, 4)
    count = 2 * group * rows

    def forward(c):
        def step(k):
            qz(c, k).wait_recv()
            qx(c, k).start()
        over(1, m, step)

    def attend(c, g):
        base = g * group
        hs = range(c * CHUNK, (c + 1) * CHUNK)
        scores = [
            lax.dot_general(
                qall[:, pl.ds(base, group), :, cols(h)].reshape(count, HEAD_DIM),
                kbuf[h], (((1,), (1,)), ((), ())), preferred_element_type=jnp.float32,
            )
            for h in hs
        ]
        for h, score in zip(hs, scores):
            peak = jnp.max(score, axis=-1, keepdims=True)
            weights = jnp.exp((score - peak) * factor)
            sums = jnp.sum(weights, axis=-1, keepdims=True)
            context = jnp.dot(
                weights.astype(jnp.bfloat16), vbuf[h], preferred_element_type=jnp.float32
            )
            local[h, :, pl.ds(base, group)] = (context / sums).reshape(2, group, rows, HEAD_DIM)
            stat[:, pl.ds(base, group), :, pl.ds(h, 1)] = (
                peak * factor + jnp.log(sums)
            ).reshape(2, group, rows, 1)

    def compute(c):
        qx_own(c).wait_recv()
        over(1, m, lambda k: qx(c, k).wait_recv())
        over(0, m // group, functools.partial(attend, c))
        for i in range(CHUNK):
            xout[c, i] = encode(local[c * CHUNK + i, other])
        x_send(c).start()
        flat = stat[other].reshape(m * rows, LANES)
        tout[c] = flat.T[: tout.shape[1]]
        t_send(c).start()

    def merge(c):
        t_send(c).wait_recv()
        flat = tin[c].T
        x_send(c).wait_recv()
        for i in range(CHUNK):
            h = c * CHUNK + i
            mine = stat[side, :, :, pl.ds(h, 1)]
            theirs = flat[:, h : h + 1].reshape(m, rows, 1)
            top = jnp.maximum(mine, theirs)
            total = top + jnp.log(jnp.exp(mine - top) + jnp.exp(theirs - top))
            value = local[h, side] * jnp.exp(mine - total) + decode(xin[c, i]) * jnp.exp(theirs - total)
            local[h, side] = value
            zstat[:, :, pl.ds(h, 1)] = total
            coded = encode(value)
            zout[c, :, i] = coded
        over(1, m, lambda k: z_send(c, k).start())

    forward(0)
    for c in range(chunks):
        if c + 1 < chunks:
            forward(c + 1)
        compute(c)
        if c > 0:
            merge(c - 1)
    merge(chunks - 1)
    over(1, m, lambda k: y_send(k).start())

    ystat[place] = zstat[place]
    over(1, m, lambda k: y_send(k).wait_recv())
    peaks = ystat[...]
    top = jnp.max(peaks, axis=0, keepdims=True)
    share = jnp.exp(peaks - top)
    share = share / jnp.sum(share, axis=0, keepdims=True)
    ystat[...] = share
    for c in range(chunks):
        over(1, m, lambda k: z_send(c, k).wait_recv())
        for i in range(CHUNK):
            h = c * CHUNK + i
            result = local[h, side, place] * ystat[place, :, pl.ds(h, 1)]
            for k in range(1, m):
                b = behind(k)
                result = result + decode(zin[c, b, i]) * ystat[b, :, pl.ds(h, 1)]
            o_ref[:, cols(h)] = result.astype(o_ref.dtype)

    for c in range(chunks):
        over(1, m, lambda k: qz(c, k).wait_send())
        qx_own(c).wait_send()
        over(1, m, lambda k: qx(c, k).wait_send())
        x_send(c).wait_send()
        t_send(c).wait_send()
        over(1, m, lambda k: z_send(c, k).wait_send())
    over(1, m, lambda k: y_send(k).wait_send())


def body(n, queries, keys, values):
    rows, columns = queries.shape
    depth = keys.shape[0]
    heads = columns // HEAD_DIM
    chunks = heads // CHUNK
    m = n // 2
    high = 8 * pl.cdiv(heads, 8)
    dma = pltpu.SemaphoreType.DMA
    vmem = pl.BlockSpec(memory_space=pltpu.VMEM)
    hbm = pl.BlockSpec(memory_space=pltpu.HBM)
    return pl.pallas_call(
        functools.partial(kernel, n),
        out_shape=jax.ShapeDtypeStruct((rows, columns), jnp.bfloat16),
        in_specs=[vmem, hbm, hbm],
        out_specs=vmem,
        scratch_shapes=[
            pltpu.VMEM((2, m, rows, columns), jnp.bfloat16),
            pltpu.VMEM((heads, depth, HEAD_DIM), jnp.bfloat16),
            pltpu.VMEM((heads, depth, HEAD_DIM), jnp.bfloat16),
            pltpu.VMEM((heads, 2, m, rows, HEAD_DIM), jnp.float32),
            pltpu.VMEM((2, m, rows, LANES), jnp.float32),
            pltpu.VMEM((chunks, CHUNK, m, rows, HEAD_DIM), LINK),
            pltpu.VMEM((chunks, CHUNK, m, rows, HEAD_DIM), LINK),
            pltpu.VMEM((chunks, high, m * rows), jnp.float32),
            pltpu.VMEM((chunks, high, m * rows), jnp.float32),
            pltpu.VMEM((chunks, m, CHUNK, rows, HEAD_DIM), LINK),
            pltpu.VMEM((chunks, m, CHUNK, rows, HEAD_DIM), LINK),
            pltpu.VMEM((m, rows, LANES), jnp.float32),
            pltpu.VMEM((m, rows, LANES), jnp.float32),
            dma((heads,)), dma((heads,)),
            dma((chunks, m)), dma((chunks, m)),
            dma((chunks, m)), dma((chunks, m)),
            dma((chunks,)), dma((chunks,)),
            dma((chunks,)), dma((chunks,)),
            dma((chunks, m)), dma((chunks, m)),
            dma((m,)), dma((m,)),
        ],
        compiler_params=pltpu.CompilerParams(
            collective_id=0, has_side_effects=True, vmem_limit_bytes=48 * 1024 * 1024
        ),
        name="attend",
    )(queries, keys, values)


def solution(mesh):
    spec = P(("groups", "seq"), "tensor")
    return jax.shard_map(
        functools.partial(body, mesh.shape["seq"]),
        mesh=mesh,
        in_specs=(spec, spec, spec),
        out_specs=spec,
        check_vma=False,
    )
```

time: 32.4 us -> 28 us (0.86)
  Pallas kernels: 28.9 us -> 24.5 us
    pallas_call x1, Pallas kernels: 28.9 us -> 24.5 us  [body(): pl.pallas_call(functools.partial(kernel, n), out_shape=jax.ShapeDtypeStru...]
where the time goes in v2:
time: 28 us; the launch traced here: 27.9 us
  Pallas kernels  24.5 us (88%)
  local copies, waits for them, and re-layouts  3.31 us (12%)
    pallas_call x1, Pallas kernels, body(): pl.pallas_call(functools.partial(kernel, n), out_shape=jax.ShapeDtypeStru...  24.5 us
    unnamed x5, local copies, waits for them, and re-layouts  3.31 us

profile of v2, /device:TPU:0, one launch (start us, length us, event | category | flops | bytes accessed | tf_op | source)
XLA Modules:
  0.0 27.9 jit_solution(17928038605000422572)
XLA Ops:
  0.0 0.0 copy-start
  0.0 1.9 %copy-done = bf16[1024,1536]{1,0:T(8,128)(2,1)S(1)} copy-done((bf16[1024,1536]{1,0:T(8,128)(2,1)S(1)}, bf16[1024,1536]{1,0:T(8,128)(2,1)}, u32[]{:S(2)}) %copy-start) | copy-done | bytes 3145752
  1.9 0.0 copy-start.1
  1.9 0.8 %copy-done.1 = bf16[16,1536]{1,0:T(8,128)(2,1)S(1)} copy-done((bf16[16,1536]{1,0:T(8,128)(2,1)S(1)}, bf16[16,1536]{1,0:T(8,128)(2,1)}, u32[]{:S(2)}) %copy-start.1) | copy-done | bytes 49176
  2.7 24.5 %attend.1 = bf16[16,1536]{1,0:T(8,128)(2,1)S(1)} custom-call(bf16[16,1536]{1,0:T(8,128)(2,1)S(1)} %copy-done.1, bf16[1024,1536]{1,0:T(8,128)(2,1)S(1)} %copy-done, bf16[1024,1536]{1,0:T(8,128)(2,1)} %v_hbm.1), custom_call_target="tpu_custom_call" | custom-call | tf_op jit(solution)/shard_map/attend/pallas_call | solution.py:235
  27.2 0.6 %copy.5 = bf16[16,1536]{1,0:T(8,128)(2,1)} copy(bf16[16,1536]{1,0:T(8,128)(2,1)S(1)} %attend.1) | data formatting | bytes 98304
Async XLA Ops:
  0.0 1.9 %copy-start = (bf16[1024,1536]{1,0:T(8,128)(2,1)S(1)}, bf16[1024,1536]{1,0:T(8,128)(2,1)}, u32[]{:S(2)}) copy-start(bf16[1024,1536]{1,0:T(8,128)(2,1)} %k_hbm.1) | copy-start | bytes 9437188
  1.9 0.8 %copy-start.1 = (bf16[16,1536]{1,0:T(8,128)(2,1)S(1)}, bf16[16,1536]{1,0:T(8,128)(2,1)}, u32[]{:S(2)}) copy-start(bf16[16,1536]{1,0:T(8,128)(2,1)} %q_ref.1) | copy-start | bytes 147460

commit v3 on v2

--- a/solution.py
+++ b/solution.py
@@ -11,7 +11,9 @@
 HEAD_DIM = 256
 LANES = 128
 LINK = jnp.bfloat16
-CHUNK = 3
+SIZES = (2, 2, 2)
+AHEAD = 2
+LAG = 3
 RAISE = 2.0**28
 LOWER = 2.0**-28
 
@@ -34,6 +36,10 @@
             step(index)
     else:
         lax.fori_loop(start, stop, lambda index, _: (step(index), 0)[1], 0)
+
+
+def split_heads(heads):
+    return SIZES if sum(SIZES) == heads else (heads,)
 
 
 def kernel(
@@ -43,7 +49,9 @@
 ):
     rows, columns = q_ref.shape
     heads = columns // HEAD_DIM
-    chunks = heads // CHUNK
+    sizes = split_heads(heads)
+    starts = [sum(sizes[:c]) for c in range(len(sizes))]
+    chunks = len(sizes)
     factor = 1.0 / math.sqrt(HEAD_DIM)
     m = n // 2
     me = lax.axis_index("seq")
@@ -62,7 +70,7 @@
         return pl.ds(h * HEAD_DIM, HEAD_DIM)
 
     def span(c):
-        return pl.ds(c * CHUNK * HEAD_DIM, CHUNK * HEAD_DIM)
+        return pl.ds(starts[c] * HEAD_DIM, sizes[c] * HEAD_DIM)
 
     def k_copy(h):
         return pltpu.make_async_copy(k_hbm.at[:, cols(h)], kbuf.at[h], ksem.at[h])
@@ -92,13 +100,15 @@
         return remote(ref, ref, qxs.at[c, k], qxr.at[c, k], pair)
 
     def x_send(c):
-        return remote(xout.at[c], xin.at[c], xs.at[c], xr.at[c], pair)
+        part = pl.ds(starts[c], sizes[c])
+        return remote(xout.at[part], xin.at[part], xs.at[c], xr.at[c], pair)
 
     def t_send(c):
         return remote(tout.at[c], tin.at[c], ts.at[c], tr.at[c], pair)
 
     def z_send(c, k):
-        return remote(zout.at[c, ahead(k)], zin.at[c, place], zs.at[c, k], zr.at[c, k], column(k))
+        part = pl.ds(starts[c], sizes[c])
+        return remote(zout.at[ahead(k), part], zin.at[place, part], zs.at[c, k], zr.at[c, k], column(k))
 
     def y_send(k):
         return remote(zstat.at[ahead(k)], ystat.at[place], ys.at[k], yr.at[k], column(k))
@@ -137,7 +147,7 @@
 
     def attend(c, g):
         base = g * group
-        hs = range(c * CHUNK, (c + 1) * CHUNK)
+        hs = range(starts[c], starts[c] + sizes[c])
         scores = [
             lax.dot_general(
                 qall[:, pl.ds(base, group), :, cols(h)].reshape(count, HEAD_DIM),
@@ -161,39 +171,41 @@
         qx_own(c).wait_recv()
         over(1, m, lambda k: qx(c, k).wait_recv())
         over(0, m // group, functools.partial(attend, c))
-        for i in range(CHUNK):
-            xout[c, i] = encode(local[c * CHUNK + i, other])
-        x_send(c).start()
         flat = stat[other].reshape(m * rows, LANES)
         tout[c] = flat.T[: tout.shape[1]]
         t_send(c).start()
+        for h in range(starts[c], starts[c] + sizes[c]):
+            xout[h] = encode(local[h, other])
+        x_send(c).start()
 
     def merge(c):
         t_send(c).wait_recv()
         flat = tin[c].T
-        x_send(c).wait_recv()
-        for i in range(CHUNK):
-            h = c * CHUNK + i
+        hs = range(starts[c], starts[c] + sizes[c])
+        shares = []
+        for h in hs:
             mine = stat[side, :, :, pl.ds(h, 1)]
             theirs = flat[:, h : h + 1].reshape(m, rows, 1)
             top = jnp.maximum(mine, theirs)
             total = top + jnp.log(jnp.exp(mine - top) + jnp.exp(theirs - top))
-            value = local[h, side] * jnp.exp(mine - total) + decode(xin[c, i]) * jnp.exp(theirs - total)
+            zstat[:, :, pl.ds(h, 1)] = total
+            shares.append((jnp.exp(mine - total), jnp.exp(theirs - total)))
+        if c == chunks - 1:
+            over(1, m, lambda k: y_send(k).start())
+        x_send(c).wait_recv()
+        for h, (mine, theirs) in zip(hs, shares):
+            value = local[h, side] * mine + decode(xin[h]) * theirs
             local[h, side] = value
-            zstat[:, :, pl.ds(h, 1)] = total
-            coded = encode(value)
-            zout[c, :, i] = coded
+            zout[:, h] = encode(value)
         over(1, m, lambda k: z_send(c, k).start())
 
-    forward(0)
-    for c in range(chunks):
-        if c + 1 < chunks:
-            forward(c + 1)
-        compute(c)
-        if c > 0:
-            merge(c - 1)
-    merge(chunks - 1)
-    over(1, m, lambda k: y_send(k).start())
+    for t in range(-AHEAD, chunks + LAG):
+        if 0 <= t + AHEAD < chunks:
+            forward(t + AHEAD)
+        if 0 <= t < chunks:
+            compute(t)
+        if 0 <= t - LAG < chunks:
+            merge(t - LAG)
 
     ystat[place] = zstat[place]
     over(1, m, lambda k: y_send(k).wait_recv())
@@ -204,12 +216,11 @@
     ystat[...] = share
     for c in range(chunks):
         over(1, m, lambda k: z_send(c, k).wait_recv())
-        for i in range(CHUNK):
-            h = c * CHUNK + i
+        for h in range(starts[c], starts[c] + sizes[c]):
             result = local[h, side, place] * ystat[place, :, pl.ds(h, 1)]
             for k in range(1, m):
                 b = behind(k)
-                result = result + decode(zin[c, b, i]) * ystat[b, :, pl.ds(h, 1)]
+                result = result + decode(zin[b, h]) * ystat[b, :, pl.ds(h, 1)]
             o_ref[:, cols(h)] = result.astype(o_ref.dtype)
 
     for c in range(chunks):
@@ -226,7 +237,7 @@
     rows, columns = queries.shape
     depth = keys.shape[0]
     heads = columns // HEAD_DIM
-    chunks = heads // CHUNK
+    chunks = len(split_heads(heads))
     m = n // 2
     high = 8 * pl.cdiv(heads, 8)
     dma = pltpu.SemaphoreType.DMA
@@ -243,12 +254,12 @@
             pltpu.VMEM((heads, depth, HEAD_DIM), jnp.bfloat16),
             pltpu.VMEM((heads, 2, m, rows, HEAD_DIM), jnp.float32),
             pltpu.VMEM((2, m, rows, LANES), jnp.float32),
-            pltpu.VMEM((chunks, CHUNK, m, rows, HEAD_DIM), LINK),
-            pltpu.VMEM((chunks, CHUNK, m, rows, HEAD_DIM), LINK),
+            pltpu.VMEM((heads, m, rows, HEAD_DIM), LINK),
+            pltpu.VMEM((heads, m, rows, HEAD_DIM), LINK),
             pltpu.VMEM((chunks, high, m * rows), jnp.float32),
             pltpu.VMEM((chunks, high, m * rows), jnp.float32),
-            pltpu.VMEM((chunks, m, CHUNK, rows, HEAD_DIM), LINK),
-            pltpu.VMEM((chunks, m, CHUNK, rows, HEAD_DIM), LINK),
+            pltpu.VMEM((m, heads, rows, HEAD_DIM), LINK),
+            pltpu.VMEM((m, heads, rows, HEAD_DIM), LINK),
             pltpu.VMEM((m, rows, LANES), jnp.float32),
             pltpu.VMEM((m, rows, LANES), jnp.float32),
             dma((heads,)), dma((heads,)),

time: 28 us -> 26.6 us (0.950)
  Pallas kernels: 24.5 us -> 23.1 us
    pallas_call x1, Pallas kernels: 24.5 us -> 23.1 us  [body(): pl.pallas_call(functools.partial(kernel, n), out_shape=jax.ShapeDtypeStru...]
where the time goes in v3:
time: 26.6 us; the launch traced here: 26.4 us
  Pallas kernels  23.1 us (87%)
  local copies, waits for them, and re-layouts  3.31 us (12%)
    pallas_call x1, Pallas kernels, body(): pl.pallas_call(functools.partial(kernel, n), out_shape=jax.ShapeDtypeStru...  23.1 us
    unnamed x5, local copies, waits for them, and re-layouts  3.31 us

profile of v3, /device:TPU:0, one launch (start us, length us, event | category | flops | bytes accessed | tf_op | source)
XLA Modules:
  0.0 26.4 jit_solution(1233629821637662345)
XLA Ops:
  0.0 0.0 copy-start
  0.0 1.9 %copy-done = bf16[1024,1536]{1,0:T(8,128)(2,1)S(1)} copy-done((bf16[1024,1536]{1,0:T(8,128)(2,1)S(1)}, bf16[1024,1536]{1,0:T(8,128)(2,1)}, u32[]{:S(2)}) %copy-start) | copy-done | bytes 3145752
  1.9 0.0 copy-start.1
  1.9 0.8 %copy-done.1 = bf16[16,1536]{1,0:T(8,128)(2,1)S(1)} copy-done((bf16[16,1536]{1,0:T(8,128)(2,1)S(1)}, bf16[16,1536]{1,0:T(8,128)(2,1)}, u32[]{:S(2)}) %copy-start.1) | copy-done | bytes 49176
  2.7 23.1 %attend.1 = bf16[16,1536]{1,0:T(8,128)(2,1)S(1)} custom-call(bf16[16,1536]{1,0:T(8,128)(2,1)S(1)} %copy-done.1, bf16[1024,1536]{1,0:T(8,128)(2,1)S(1)} %copy-done, bf16[1024,1536]{1,0:T(8,128)(2,1)} %v_hbm.1), custom_call_target="tpu_custom_call" | custom-call | tf_op jit(solution)/shard_map/attend/pallas_call | solution.py:246
  25.8 0.6 %copy.5 = bf16[16,1536]{1,0:T(8,128)(2,1)} copy(bf16[16,1536]{1,0:T(8,128)(2,1)S(1)} %attend.1) | data formatting | bytes 98304
Async XLA Ops:
  0.0 1.9 %copy-start = (bf16[1024,1536]{1,0:T(8,128)(2,1)S(1)}, bf16[1024,1536]{1,0:T(8,128)(2,1)}, u32[]{:S(2)}) copy-start(bf16[1024,1536]{1,0:T(8,128)(2,1)} %k_hbm.1) | copy-start | bytes 9437188
  1.9 0.8 %copy-start.1 = (bf16[16,1536]{1,0:T(8,128)(2,1)S(1)}, bf16[16,1536]{1,0:T(8,128)(2,1)}, u32[]{:S(2)}) copy-start(bf16[16,1536]{1,0:T(8,128)(2,1)} %q_ref.1) | copy-start | bytes 147460

commit v4 on v3

--- a/solution.py
+++ b/solution.py
@@ -130,7 +130,7 @@
     pl.semaphore_wait(barrier, m)
 
     for c in range(chunks):
-        over(1, m, lambda k: qz(c, k).start())
+        over(1, m, lambda k: qz(c, m - k).start())
         qx_own(c).start()
     for h in range(heads):
         k_copy(h).wait()

time: 26.6 us -> 26.3 us (0.989)
  Pallas kernels: 23.1 us -> 22.8 us
    pallas_call x1, Pallas kernels: 23.1 us -> 22.8 us  [body(): pl.pallas_call(functools.partial(kernel, n), out_shape=jax.ShapeDtypeStru...]
where the time goes in v4:
time: 26.3 us; the launch traced here: 26.1 us
  Pallas kernels  22.8 us (87%)
  local copies, waits for them, and re-layouts  3.31 us (13%)
    pallas_call x1, Pallas kernels, body(): pl.pallas_call(functools.partial(kernel, n), out_shape=jax.ShapeDtypeStru...  22.8 us
    unnamed x5, local copies, waits for them, and re-layouts  3.31 us

profile of v4, /device:TPU:0, one launch (start us, length us, event | category | flops | bytes accessed | tf_op | source)
XLA Modules:
  0.0 26.1 jit_solution(2878899928400518260)
XLA Ops:
  0.0 0.0 copy-start
  0.0 1.9 %copy-done = bf16[1024,1536]{1,0:T(8,128)(2,1)S(1)} copy-done((bf16[1024,1536]{1,0:T(8,128)(2,1)S(1)}, bf16[1024,1536]{1,0:T(8,128)(2,1)}, u32[]{:S(2)}) %copy-start) | copy-done | bytes 3145752
  1.9 0.0 copy-start.1
  1.9 0.8 %copy-done.1 = bf16[16,1536]{1,0:T(8,128)(2,1)S(1)} copy-done((bf16[16,1536]{1,0:T(8,128)(2,1)S(1)}, bf16[16,1536]{1,0:T(8,128)(2,1)}, u32[]{:S(2)}) %copy-start.1) | copy-done | bytes 49176
  2.7 22.8 %attend.1 = bf16[16,1536]{1,0:T(8,128)(2,1)S(1)} custom-call(bf16[16,1536]{1,0:T(8,128)(2,1)S(1)} %copy-done.1, bf16[1024,1536]{1,0:T(8,128)(2,1)S(1)} %copy-done, bf16[1024,1536]{1,0:T(8,128)(2,1)} %v_hbm.1), custom_call_target="tpu_custom_call" | custom-call | tf_op jit(solution)/shard_map/attend/pallas_call | solution.py:246
  25.5 0.6 %copy.5 = bf16[16,1536]{1,0:T(8,128)(2,1)} copy(bf16[16,1536]{1,0:T(8,128)(2,1)S(1)} %attend.1) | data formatting | bytes 98304
Async XLA Ops:
  0.0 1.9 %copy-start = (bf16[1024,1536]{1,0:T(8,128)(2,1)S(1)}, bf16[1024,1536]{1,0:T(8,128)(2,1)}, u32[]{:S(2)}) copy-start(bf16[1024,1536]{1,0:T(8,128)(2,1)} %k_hbm.1) | copy-start | bytes 9437188
  1.9 0.8 %copy-start.1 = (bf16[16,1536]{1,0:T(8,128)(2,1)S(1)}, bf16[16,1536]{1,0:T(8,128)(2,1)}, u32[]{:S(2)}) copy-start(bf16[16,1536]{1,0:T(8,128)(2,1)} %q_ref.1) | copy-start | bytes 147460
